TPU v7x, 512 devices: a whole 4x4x16 slice. The times are simulated.
512 devices in a mesh: gx: 32 (over z_lo, y, core), gy: 16 (over x, z_hi).
Axes of the slice: x: 4, y: 4, z: 16 (z_hi: 4, z_lo: 4; z = z_hi * 4 + z_lo), core: 2. Of those that a mesh axis runs over, the one named last changes fastest.
Arguments:
- deflation: float32 [32, 320, 80, 128], P(None, 'gx', 'gy'), may hold values from -13 to 13
- layers: int32 [256, 48, 128], P('gx', 'gy'), may hold values from 0 to 84
- layer_table: float32 [85], replicated, may hold values from 0.02 to 2
- forcing: float32 [256, 48, 128], P('gx', 'gy'), may hold values from -13 to 13
Outputs:
- coarse_rows: float32 [32, 16, 9, 32, 32], P('gx', 'gy')
- coarse_solution: float32 [32, 16, 32], P('gx', 'gy')
All inputs are finite; a program needn't handle non-finite values.
Results may differ from a plain program's by a relative error of at most 0.0003.
Values sent between devices are 32-bit elements; how exact they have to be, the bound alone decides.
A program may use at most 64 MiB of HBM per device.

v0:
```python
import math

import jax
import jax.numpy as jnp
from jax import lax
from jax.sharding import PartitionSpec as P

VEC = 32
CX = 8
CY = 3
CZ = 128
MARGIN = 1
LAYERS = 85
ITERS = 3
EX = 10
EY = 5


storage_term = 0.5
upper_offsets = ((0, 0), (0, 1), (1, -1), (1, 0), (1, 1))


def extended(value, sides, width):
    for axis, dim in sides:
        devices, length = (lax.axis_size(axis), value.shape[dim])
        up = [(i, (i + 1) % devices) for i in range(devices - 1)]
        down = [(j, i) for i, j in up]
        last = lax.slice_in_dim(value, length - width, length, axis=dim)
        initial = lax.slice_in_dim(value, 0, width, axis=dim)
        before = lax.ppermute(last, axis, up)
        after = lax.ppermute(initial, axis, down)
        value = jnp.concatenate([before, value, after], axis=dim)
    return value


def unity_weights(index_pos, subdomains, own_cells):
    offset = jnp.arange(own_cells + 2 * MARGIN, dtype=jnp.int32)
    global_pos = index_pos * own_cells - MARGIN + offset
    inside = ((global_pos >= 0) & (global_pos < subdomains * own_cells)).astype(jnp.float32)
    below_side = ((index_pos > 0) & (global_pos < index_pos * own_cells + MARGIN)).astype(
        jnp.float32
    )
    above_side = (
        (index_pos < subdomains - 1) & (global_pos >= (index_pos + 1) * own_cells - MARGIN)
    ).astype(jnp.float32)
    return inside / (1.0 + below_side + above_side)


def operate(padded, kappa_box):
    centre = padded[:, 1:-1, 1:-1]
    kappa_centre = kappa_box[1:-1, 1:-1]
    width_x = centre.shape[1]
    width_y = centre.shape[2]
    result = storage_term * centre
    for shift_x, shift_y in ((1, 0), (-1, 0), (0, 1), (0, -1)):
        beside = padded[:, 1 + shift_x : 1 + shift_x + width_x, 1 + shift_y : 1 + shift_y + width_y]
        kappa_beside = kappa_box[
            1 + shift_x : 1 + shift_x + width_x, 1 + shift_y : 1 + shift_y + width_y
        ]
        result = result + jnp.sqrt(kappa_centre * kappa_beside) * (centre - beside)
    for forward in (True, False):
        if forward:
            beside = jnp.pad(centre[..., 1:], ((0, 0), (0, 0), (0, 0), (0, 1)))
            kappa_beside = jnp.pad(kappa_centre[..., 1:], ((0, 0), (0, 0), (0, 1)))
        else:
            beside = jnp.pad(centre[..., :-1], ((0, 0), (0, 0), (0, 0), (1, 0)))
            kappa_beside = jnp.pad(kappa_centre[..., :-1], ((0, 0), (0, 0), (1, 0)))
        result = result + jnp.sqrt(kappa_centre * kappa_beside) * (centre - beside)
    return result


def strip_bounds(shift, ext_cells):
    slab_depth = 2 * MARGIN + 1
    if shift < 0:
        return (0, 0, slab_depth)
    if shift == 0:
        return (slab_depth, 1, ext_cells)
    return (slab_depth + ext_cells, ext_cells + 2 - slab_depth, slab_depth)


def block_with(applied, strip, shift_x, shift_y):
    unused_x, start_bx, length_x = strip_bounds(shift_x, EX)
    unused_y, start_by, length_y = strip_bounds(shift_y, EY)
    region = applied[:, start_bx : start_bx + length_x, start_by : start_by + length_y]
    return jnp.dot(
        region.reshape(VEC, -1), strip.reshape(VEC, -1).T, precision=lax.Precision.HIGHEST
    )


def conjugate(coarse_load, image_of, total_of):
    solution = jnp.zeros_like(coarse_load)
    residual = coarse_load
    direction = coarse_load
    norm_now = total_of(jnp.sum(residual * residual))
    for iteration in range(ITERS):
        mapped = image_of(direction)
        step_size = norm_now / total_of(jnp.sum(direction * mapped))
        solution = solution + step_size * direction
        residual = residual - step_size * mapped
        norm_next = total_of(jnp.sum(residual * residual))
        direction = residual + norm_next / norm_now * direction
        norm_now = norm_next
    return solution


def plain_total(value):
    return value


def take_from(vector, offset, reach):
    count = vector.shape[1]
    padded_vec = jnp.pad(vector, ((0, 0), (reach, reach)))
    return padded_vec[:, reach + offset : reach + offset + count]


def half_product(upper_rows, vector, mesh_x, mesh_y):
    count = vector.shape[1]
    reach = mesh_y + 1
    flat = jnp.arange(count, dtype=jnp.int32)
    place_x = flat // mesh_y
    place_y = flat % mesh_y
    result = jnp.zeros_like(vector)
    spread = jnp.zeros_like(vector)
    for slot_index in range(len(upper_offsets)):
        shift_x, shift_y = upper_offsets[slot_index]
        offset = shift_x * mesh_y + shift_y
        valid = (
            (place_x + shift_x >= 0)
            & (place_x + shift_x < mesh_x)
            & (place_y + shift_y >= 0)
            & (place_y + shift_y < mesh_y)
        ).astype(jnp.float32)
        coarse_block = upper_rows[slot_index]
        moved = take_from(vector, offset, reach) * valid[None, :]
        result = result + jnp.sum(coarse_block * moved[None, :, :], axis=1)
        if shift_x != 0 or shift_y != 0:
            sent_back = jnp.sum(coarse_block * vector[:, None, :], axis=0) * valid[None, :]
            spread = spread + take_from(sent_back, -offset, reach)
    return result + spread


def body(deflation, layers, layer_table, forcing):
    mesh_x = lax.axis_size("gx")
    mesh_y = lax.axis_size("gy")
    index_x = lax.axis_index("gx")
    index_y = lax.axis_index("gy")
    slab_depth = 2 * MARGIN + 1
    onehot = (layers.reshape(1, -1) == jnp.arange(LAYERS, dtype=jnp.int32)[:, None]).astype(
        jnp.float32
    )
    permeability = jnp.dot(layer_table, onehot, precision=lax.Precision.HIGHEST).reshape(CX, CY, CZ)
    fields = jnp.stack([permeability, forcing])
    rimmed = extended(fields, (("gx", 1), ("gy", 2)), MARGIN + 1)
    weights = (
        unity_weights(index_x, mesh_x, CX)[:, None, None]
        * unity_weights(index_y, mesh_y, CY)[None, :, None]
    )
    basis = deflation * weights * (1.0 / math.sqrt(CX * CY * CZ))
    kappa_box = jnp.pad(rimmed[0], ((1, 1), (1, 1), (0, 0)))
    forcing_ext = rimmed[1, 1:-1, 1:-1]
    applied = operate(jnp.pad(basis, ((0, 0), (2, 2), (2, 2), (0, 0))), kappa_box)
    coarse_load = jnp.dot(
        basis.reshape(VEC, -1), forcing_ext.reshape(-1), precision=lax.Precision.HIGHEST
    )
    beside_all = extended(basis, (("gx", 1), ("gy", 2)), slab_depth)
    blocks = []
    for shift_x in (-1, 0, 1):
        for shift_y in (-1, 0, 1):
            start_nx, unused_bx, length_x = strip_bounds(shift_x, EX)
            start_ny, unused_by, length_y = strip_bounds(shift_y, EY)
            strip = beside_all[:, start_nx : start_nx + length_x, start_ny : start_ny + length_y]
            blocks.append(block_with(applied, strip, shift_x, shift_y))
    coarse_rows = jnp.stack(blocks)
    gathered_rows, gathered_load = (
        lax.all_gather(coarse_rows[4:].reshape(1, 5 * VEC * VEC), ("gx", "gy"), axis=0, tiled=True),
        lax.all_gather(coarse_load.reshape(1, VEC), ("gx", "gy"), axis=0, tiled=True),
    )
    upper_rows = gathered_rows.T.reshape(5, VEC, VEC, mesh_x * mesh_y)
    whole_load = gathered_load.T

    def image_all(vector):
        return half_product(upper_rows, vector, mesh_x, mesh_y)

    whole_solution = conjugate(whole_load, image_all, plain_total)
    flat_index = index_x * mesh_y + index_y
    solution = lax.dynamic_slice(whole_solution, (jnp.int32(0), flat_index), (VEC, 1)).reshape(
        1, 1, VEC
    )
    return (coarse_rows[None, None], solution)


def solution(mesh):
    return jax.shard_map(
        body,
        mesh=mesh,
        in_specs=(P(None, "gx", "gy", None), P("gx", "gy", None), P(), P("gx", "gy", None)),
        out_specs=(P("gx", "gy", None, None, None), P("gx", "gy", None)),
        check_vma=False,
    )
```

profile of v0, /device:TPU:1, one launch (start us, length us, event | category | flops | bytes accessed | tf_op | source)
XLA Modules:
  0.0 2028.3 jit_solution(9259440537845964551)
XLA Ops:
  9.2 8.8 collective-permute-start.1
  17.9 1.9 collective-permute-start
  20.0 1.3 multiply_multiply_fusion
  22.1 2.4 collective-permute-start.5
  24.5 3.2 collective-permute-start.4
  28.4 1.3 collective-permute-start.3
  29.7 8.5 collective-permute-start.2
  38.2 1.5 pad_slice_fusion.1
  40.2 1.2 reshape.203
  42.2 1.9 convolution_bitcast_fusion.9
  45.9 1.2 pad_maximum_fusion
  47.3 5.8 collective-permute-start.6
  53.3 1.3 collective-permute-start.7
  54.6 1.1 fusion.7
  55.7 21.7 %collective-permute-done.6 = f32[32,16,3,128]{3,0,2,1:T(8,128)S(1)} collective-permute-done((f32[32,16,3,128]{3,0,2,1:T(8,128)S(1)}, f32[32,16,3,128]{3,0,2,1:T(8,128)S(1)}, u32[]{:S(2)}, u32[]{:S(2)}) %collective-permute-start.6) | collective-permute-done | bytes 786464 | tf_op jit(solution)/shard_map/ppermute | solution.py:30
  77.7 1.3 fusion.16
  79.0 49.9 %collective-permute-done.7 = f32[32,16,3,128]{3,0,2,1:T(8,128)S(1)} collective-permute-done((f32[32,16,3,128]{3,0,2,1:T(8,128)S(1)}, f32[32,16,3,128]{3,0,2,1:T(8,128)S(1)}, u32[]{:S(2)}, u32[]{:S(2)}) %collective-permute-start.7) | collective-permute-done | bytes 786464 | tf_op jit(solution)/shard_map/ppermute | solution.py:31
  131.3 1.3 constant_dynamic-update-slice_fusion.6
  133.7 404.1 %all-reduce.24.cloned.1.call-done = f32[16384]{0:T(1024)} async-done(((f32[16384]{0:T(1024)}), f32[16384]{0:T(1024)}) %all-reduce.24.cloned.1.call-update) | async-done | bytes 65552
  537.7 0.9 reshape.207
  538.8 1417.8 %all-gather.4.cloned.1.call-done = f32[512,1,5120]{2,1,0:T(1,128)} async-done(((f32[1,1,5120]{2,1,0:T(1,128)}), f32[512,1,5120]{2,1,0:T(1,128)}) %all-gather.4.cloned.1.call-update) | async-done | bytes 10485776 | tf_op jit(solution)/shard_map/all_gather | solution.py:175
  1956.6 22.0 %copy.43 = f32[512,1,5120]{0,2,1:T(8,128)} copy(f32[512,1,5120]{2,1,0:T(1,128)} %all-gather.4.cloned.1.call-done) | data formatting | bytes 20971520 | tf_op jit(solution)/shard_map/all_gather | solution.py:175
  1978.6 4.7 fusion.83
  1983.3 1.1 multiply_reduce_fusion.18
  1984.6 0.8 copy-done.2
  1985.4 1.0 copy-done.3
  1986.6 1.3 slice-done.2
  1987.9 2.1 multiply_reduce_fusion.25
  1993.9 4.1 multiply_reduce_fusion.9
  1998.1 6.3 multiply_reduce_fusion.16
  2008.2 4.1 multiply_reduce_fusion
  2012.5 6.3 multiply_reduce_fusion.7
  (76 shorter events, 15.6 us)
Async XLA Ops:
  7.2 1.5 copy-start
  7.2 530.6 %all-reduce.24.cloned.1.call-start = ((), (), s32[]{:S(2)}) async-start(), calls=%async_computation | async-start | bytes 131072
  9.2 18.5 collective-permute-start.1
  17.9 9.8 collective-permute-start
  22.1 23.7 %collective-permute-start.5 = (f32[32,3,5,128]{3,0,2,1:T(8,128)}, f32[32,3,5,128]{3,0,2,1:T(8,128)}, u32[]{:S(2)}, u32[]{:S(2)}) collective-permute-start(f32[32,3,5,128]{3,0,2,1:T(8,128)} %get-tuple-element.47), channel_id=1, source_target_pairs={{16,0},{32,16},{48,32},{64,48},{80,64},{96,80},{112,96},{128,112},... | collective-permute-start | bytes 737288 | tf_op jit(solution)/shard_map/ppermute | solution.py:31
  24.5 21.4 %collective-permute-start.4 = (f32[32,3,5,128]{3,0,2,1:T(8,128)}, f32[32,3,5,128]{3,0,2,1:T(8,128)}, u32[]{:S(2)}, u32[]{:S(2)}) collective-permute-start(f32[32,3,5,128]{3,0,2,1:T(8,128)} %get-tuple-element.46), channel_id=1, source_target_pairs={{0,16},{16,32},{32,48},{48,64},{64,80},{80,96},{96,112},{112,128},... | collective-permute-start | bytes 737288 | tf_op jit(solution)/shard_map/ppermute | solution.py:30
  27.7 2.0 copy-start.6
  28.4 13.0 collective-permute-start.3
  29.7 11.7 collective-permute-start.2
  44.4 0.6 copy-start.5
  45.0 1911.6 %all-gather.4.cloned.1.call-start = ((), (), s32[]{:S(2)}) async-start(), calls=%async_computation.1 | async-start | bytes 10506240 | tf_op jit(solution)/shard_map/all_gather | solution.py:175
  47.1 7.5 copy-start.4
  47.3 30.1 %collective-permute-start.6 = (f32[32,16,3,128]{3,0,2,1:T(8,128)S(1)}, f32[32,16,3,128]{3,0,2,1:T(8,128)S(1)}, u32[]{:S(2)}, u32[]{:S(2)}) collective-permute-start(f32[32,16,3,128]{3,0,2,1:T(8,128)S(1)} %get-tuple-element.45), channel_id=1, source_target_pairs={{0,1},{1,2},{2,3},{3,4},{4,5},{5,6},{6,7},{7,8},{8,9},{9,10},{10,1... | collective-permute-start | bytes 2359304 | tf_op jit(solution)/shard_map/ppermute | solution.py:30
  53.3 75.6 %collective-permute-start.7 = (f32[32,16,3,128]{3,0,2,1:T(8,128)S(1)}, f32[32,16,3,128]{3,0,2,1:T(8,128)S(1)}, u32[]{:S(2)}, u32[]{:S(2)}) collective-permute-start(f32[32,16,3,128]{3,0,2,1:T(8,128)S(1)} %get-tuple-element.44), channel_id=1, source_target_pairs={{1,0},{2,1},{3,2},{4,3},{5,4},{6,5},{7,6},{8,7},{9,8},{10,9},{11,1... | collective-permute-start | bytes 2359304 | tf_op jit(solution)/shard_map/ppermute | solution.py:31
  132.9 1845.7 %copy-start.7 = (f32[9,32,32]{2,1,0:T(8,128)}, f32[9,32,32]{2,1,0:T(8,128)S(1)}, u32[]{:S(2)}) copy-start(f32[9,32,32]{2,1,0:T(8,128)S(1)} %get-tuple-element.75) | copy-start | bytes 110596
  1978.6 8.0 slice-start
  1978.6 8.0 slice-start.1
  1983.3 1.3 copy-start.1
  1983.3 2.1 copy-start.2
  1983.3 3.1 copy-start.3
  1983.3 4.5 slice-start.2
Sparse Core Ops, SparseCore 0:
  45.1 492.5 all-reduce.23
  540.2 1416.3 all-gather.3
where the time goes:
time: 2030 us
  waiting for transfers between devices  1890 us (93%)
  local copies, waits for them, and re-layouts  39 us (2%)
  other arithmetic  33.9 us (2%)
  starting transfers between devices  33.2 us (2%)
  between operations  20.8 us (1%)
    all_gather x1, waiting for transfers between devices, body(): lax.all_gather(coarse_rows[4:].reshape(1, 5 * VEC * VEC), ('gx', 'gy'), a...  1420 us
    unnamed x3, waiting for transfers between devices  404 us
    ppermute x4, waiting for transfers between devices, extended(): after = lax.ppermute(initial, axis, down)  49.9 us
  transfers between devices with their start and end apart: 10, of which 4 were waited for; matrix products, arithmetic and copies ran while one was open for 1% of the time, Pallas kernels for 0%

commit v1 on v0

v1 whole, which is shorter than its diff:
```python
import functools
import math

import jax
import jax.numpy as jnp
from jax import lax
from jax.experimental import pallas as pl
from jax.experimental.pallas import tpu as pltpu
from jax.sharding import PartitionSpec as P

VEC = 32
CX = 8
CY = 3
CZ = 128
MARGIN = 1
LAYERS = 85
ITERS = 3
EX = 10
EY = 5
MESH = pl.DeviceIdType.MESH
F32 = jnp.float32
BF16 = jnp.bfloat16

EDGE = (0, 1, 2, 7, 8, 9)
DIRS = ((1, 0), (-1, 0), (0, 1), (0, -1), (1, 1), (-1, 1), (1, -1), (-1, -1))
SEND_X = {1: (8, 2), -1: (2, 2), 0: (2, 8)}
LAND_X = {1: (0, 2), -1: (10, 2), 0: (2, 8)}
SEND_Y = {1: (3, 2), -1: (2, 2), 0: (2, 3)}
LAND_Y = {1: (0, 2), -1: (5, 2), 0: (2, 3)}


def unity_weights(index_pos, subdomains, own_cells):
    offset = jnp.arange(own_cells + 2 * MARGIN, dtype=jnp.int32)
    global_pos = index_pos * own_cells - MARGIN + offset
    inside = ((global_pos >= 0) & (global_pos < subdomains * own_cells)).astype(F32)
    below_side = ((index_pos > 0) & (global_pos < index_pos * own_cells + MARGIN)).astype(F32)
    above_side = (
        (index_pos < subdomains - 1) & (global_pos >= (index_pos + 1) * own_cells - MARGIN)
    ).astype(F32)
    return inside / (1.0 + below_side + above_side)


def pack(cells):
    highs = [c.astype(BF16) for c in cells]
    lows = [(c - h.astype(F32)).astype(BF16) for c, h in zip(cells, highs)]
    high = jnp.concatenate(highs, axis=1)
    low = jnp.concatenate(lows, axis=1)
    return jnp.concatenate([high, low], axis=0)


def dot_cells(left, right):
    return lax.dot_general(
        pack(left), pack(right), (((1,), (1,)), ((), ())), preferred_element_type=F32
    )


def fold(wide):
    tall = wide[0:VEC] + wide[VEC:]
    return tall[:, 0:VEC] + tall[:, VEC:]


def squeeze_block(block):
    return jnp.concatenate([block[8 * g : 8 * g + 8] for g in range(4)], axis=1)


def spread_block(packed):
    return jnp.concatenate([packed[:, VEC * g : VEC * g + VEC] for g in range(4)], axis=0)


def kernel(
    nx, ny, basis, layers, table, forcing, rows, answer,
    field, weighted, image, strip_x, strip_y, strip_m, corner_r, corner_l,
    block_out, block_in, vec_out, vec_in, sum_out, sum_x, sum_y,
    f_send, f_recv, y_send, y_recv, s_send, s_recv, c_send, c_recv,
    b_send, b_recv, v_send, v_recv, a_send, a_recv,
):
    px = lax.axis_index("gx")
    py = lax.axis_index("gy")
    right, left = lax.rem(px + 1, nx), lax.rem(px + nx - 1, nx)
    upper, lower = lax.rem(py + 1, ny), lax.rem(py + ny - 1, ny)
    at_x = {1: right, -1: left, 0: px}
    at_y = {1: upper, -1: lower, 0: py}

    def remote(src, dst, send, recv, to):
        return pltpu.make_async_remote_copy(
            src_ref=src, dst_ref=dst, send_sem=send, recv_sem=recv, device_id=to, device_id_type=MESH
        )

    barrier = pltpu.get_barrier_semaphore()

    def greet_x(k, carry):
        pl.semaphore_signal(barrier, inc=1, device_id=(lax.rem(px + k, nx), py), device_id_type=MESH)
        return carry

    def greet_y(k, carry):
        pl.semaphore_signal(barrier, inc=1, device_id=(px, lax.rem(py + k, ny)), device_id_type=MESH)
        return carry

    lax.fori_loop(1, nx, greet_x, 0)
    lax.fori_loop(1, ny, greet_y, 0)
    for dx, dy in DIRS[4:]:
        pl.semaphore_signal(barrier, inc=1, device_id=(at_x[dx], at_y[dy]), device_id_type=MESH)

    entry = layers[...]

    def look_up(t, root):
        return jnp.where(entry == t, table[t], root)

    root = jnp.sqrt(lax.fori_loop(0, LAYERS, look_up, jnp.zeros((CX, CY, CZ), F32)))
    for x in range(CX):
        for y in range(CY):
            field[2 + x, 2 + y, 0:1, :] = root[x, y : y + 1, :]
            field[2 + x, 2 + y, 1:2, :] = forcing[x, y : y + 1, :]

    pl.semaphore_wait(barrier, nx + ny + 2)

    field_copies = []
    for n, (dx, dy) in enumerate(DIRS):
        sx, lx = SEND_X[dx]
        sy, ly = SEND_Y[dy]
        tx = LAND_X[dx][0]
        ty = LAND_Y[dy][0]
        field_copies.append(
            remote(
                field.at[pl.ds(sx, lx), pl.ds(sy, ly)],
                field.at[pl.ds(tx, lx), pl.ds(ty, ly)],
                f_send.at[n], f_recv.at[n], (at_x[dx], at_y[dy]),
            )
        )
        field_copies[-1].start()
    strip_copies = [
        remote(
            basis.at[ex, pl.ds(0, 3)], strip_y.at[n], y_send.at[n], y_recv.at[n], (px, lower)
        )
        for n, ex in enumerate(EDGE)
    ]
    for n in (0, 5, 1, 4, 2, 3):
        strip_copies[n].start()
    x_copy = remote(basis.at[pl.ds(0, 3)], strip_x, s_send.at[0], s_recv.at[0], (left, py))
    x_copy.start()

    empty = jnp.zeros((VEC, CZ), F32)
    for j in range(7):
        weighted[0, j] = empty
        weighted[11, j] = empty

    def zero_rows(i, carry):
        weighted[i, 0] = empty
        weighted[i, 6] = empty
        return carry

    lax.fori_loop(1, 11, zero_rows, 0)

    for copy in field_copies:
        copy.wait_recv()
    for copy in field_copies:
        copy.wait_send()

    @pl.when(px == 0)
    def _():
        field[0:2] = jnp.zeros((2, 7, 2, CZ), F32)

    @pl.when(px == nx - 1)
    def _():
        field[10:12] = jnp.zeros((2, 7, 2, CZ), F32)

    @pl.when(py == 0)
    def _():
        field[:, 0:2] = jnp.zeros((12, 2, 2, CZ), F32)

    @pl.when(py == ny - 1)
    def _():
        field[:, 5:7] = jnp.zeros((12, 2, 2, CZ), F32)

    lane1 = lax.broadcasted_iota(jnp.int32, (1, CZ), 1)
    lane32 = lax.broadcasted_iota(jnp.int32, (VEC, CZ), 1)

    def beside(value, lane):
        before = jnp.where(lane > 0, pltpu.roll(value, 1, 1), 0.0)
        after = jnp.where(lane < CZ - 1, pltpu.roll(value, CZ - 1, 1), 0.0)
        return before + after

    def scale(i, load):
        for j in range(1, 6):
            value = basis[i - 1, j - 1]
            weighted[i, j] = field[i, j, 0:1, :] * value
            load = load + field[i, j, 1:2, :] * value
        return load

    load = lax.fori_loop(1, 11, scale, empty)

    def image_inside(i, j):
        own = field[i, j, 0:1, :]
        near = (
            field[i - 1, j, 0:1, :] + field[i + 1, j, 0:1, :]
            + field[i, j - 1, 0:1, :] + field[i, j + 1, 0:1, :] + beside(own, lane1)
        )
        total = (
            weighted[i - 1, j] + weighted[i + 1, j] + weighted[i, j - 1] + weighted[i, j + 1]
            + beside(weighted[i, j], lane32)
        )
        image[i, j] = (0.5 + own * near) * basis[i - 1, j - 1] - own * total

    def image_above(i):
        image[i, 6] = -(field[i, 6, 0:1, :] * weighted[i, 5])

    def upper_rows(i, carry):
        image_inside(i, 4)
        image_inside(i, 5)
        image_above(i)
        return carry

    def lower_rows(i, carry):
        for j in (1, 2, 3):
            image_inside(i, j)
        return carry

    lax.fori_loop(4, 8, upper_rows, 0)
    m_copy = remote(
        image.at[pl.ds(4, 4), pl.ds(4, 3)], strip_m, s_send.at[1], s_recv.at[1], (px, upper)
    )
    m_copy.start()

    row_id = lax.broadcasted_iota(jnp.int32, (VEC, VEC), 0)
    col_id = lax.broadcasted_iota(jnp.int32, (VEC, VEC), 1)
    diagonal = row_id == col_id
    blank = jnp.zeros((1, CZ - VEC), F32)

    def as_row(column):
        return jnp.sum(jnp.where(diagonal, column, 0.0), axis=0, keepdims=True)

    def vec_copies(step):
        return [
            remote(
                vec_out.at[step], vec_in.at[step, n],
                v_send.at[step, n], v_recv.at[step, n], (at_x[dx], at_y[dy]),
            )
            for n, (dx, dy) in enumerate(DIRS)
        ]

    copies = [vec_copies(step) for step in range(ITERS)]

    def send_vector(step, value):
        vec_out[step] = jnp.concatenate([value, blank], axis=1)
        for copy in copies[step]:
            copy.start()

    load_row = as_row(jnp.sum(load, axis=1, keepdims=True))
    send_vector(0, load_row)

    lax.fori_loop(1, 4, upper_rows, 0)
    lax.fori_loop(8, 11, upper_rows, 0)
    lax.fori_loop(1, 11, lower_rows, 0)
    for j in (4, 5):
        image[0, j] = -(field[0, j, 0:1, :] * weighted[1, j])
    image[0, 6] = empty
    image[11, 6] = empty
    for j in range(1, 6):
        image[11, j] = -(field[11, j, 0:1, :] * weighted[10, j])

    def own_block(t, total):
        i = 1 + 2 * t
        cells = [(i + k, j) for k in (0, 1) for j in range(1, 6)]
        return total + dot_cells(
            [image[a, b] for a, b in cells], [basis[a - 1, b - 1] for a, b in cells]
        )

    rows[4] = fold(lax.fori_loop(0, 5, own_block, jnp.zeros((2 * VEC, 2 * VEC), F32)))

    def send_block(n, block, to):
        block_out[n] = squeeze_block(block)
        copy = remote(block_out.at[n], block_in.at[n], b_send.at[n], b_recv.at[n], to)
        copy.start()
        return copy

    x_copy.wait()
    block_x = fold(
        dot_cells(
            [image[9 + k, 1 + j] for k in range(3) for j in range(EY)],
            [strip_x[k, j] for k in range(3) for j in range(EY)],
        )
    )
    rows[7] = jnp.where(px < nx - 1, block_x, 0.0)
    block_copies = [send_block(0, block_x.T, (right, py))]

    corner_copies = {}
    for n in (0, 5, 1, 4, 2, 3):
        strip_copies[n].wait()
        if n < 3:
            copy = remote(strip_y.at[n], corner_r.at[n], c_send.at[n], c_recv.at[n], (left, py))
        else:
            copy = remote(strip_y.at[n], corner_l.at[n - 3], c_send.at[n], c_recv.at[n], (right, py))
        copy.start()
        corner_copies[n] = copy

    m_copy.wait()
    part_m = fold(
        dot_cells(
            [strip_m[k, j] for k in range(4) for j in range(3)],
            [basis[3 + k, j] for k in range(4) for j in range(3)],
        )
    )
    block_copies.append(send_block(1, part_m, (px, lower)))
    part_e = fold(
        dot_cells(
            [image[1 + k, 4 + j] for k in range(3) for j in range(3)],
            [strip_y[k, j] for k in range(3) for j in range(3)],
        )
        + dot_cells(
            [image[8 + k, 4 + j] for k in range(3) for j in range(3)],
            [strip_y[3 + k, j] for k in range(3) for j in range(3)],
        )
    )
    block_copies.append(send_block(2, part_e.T, (px, upper)))
    for n in range(3):
        corner_copies[n].wait()
    block_r = fold(
        dot_cells(
            [image[9 + k, 4 + j] for k in range(3) for j in range(3)],
            [corner_r[k, j] for k in range(3) for j in range(3)],
        )
    )
    block_copies.append(send_block(3, block_r.T, (right, upper)))
    for n in range(3, 6):
        corner_copies[n].wait()
    block_l = fold(
        dot_cells(
            [image[k, 4 + j] for k in range(3) for j in range(3)],
            [corner_l[k, j] for k in range(3) for j in range(3)],
        )
    )
    block_copies.append(send_block(4, block_l.T, (left, upper)))
    has_up, has_down = py < ny - 1, py > 0
    has_right, has_left = px < nx - 1, px > 0
    rows[8] = jnp.where(has_right & has_up, block_r, 0.0)
    rows[2] = jnp.where(has_left & has_up, block_l, 0.0)
    for copy in block_copies:
        copy.wait()
    rows[1] = jnp.where(has_left, spread_block(block_in[0]), 0.0)
    rows[5] = jnp.where(has_up, part_e + spread_block(block_in[1]), 0.0)
    rows[3] = jnp.where(has_down, part_m.T + spread_block(block_in[2]), 0.0)
    rows[0] = jnp.where(has_left & has_down, spread_block(block_in[3]), 0.0)
    rows[6] = jnp.where(has_right & has_down, spread_block(block_in[4]), 0.0)

    def product(step, own):
        for copy in copies[step]:
            copy.wait()
        total = rows[4] * own
        for n, (dx, dy) in enumerate(DIRS):
            total = total + rows[3 * (1 - dx) + 1 - dy] * vec_in[step, n][:, 0:VEC]
        return as_row(jnp.sum(total, axis=1, keepdims=True))

    def summed(step, values):
        value = jnp.concatenate(values + [jnp.zeros((1, CZ - len(values)), F32)], axis=1)
        for stage, count, inbox in ((0, nx, sum_x), (1, ny, sum_y)):
            sum_out[step, stage] = value
            send, recv = a_send.at[step, stage], a_recv.at[step, stage]

            def tell(k, carry, stage=stage, inbox=inbox, send=send, recv=recv):
                to = (lax.rem(px + k, nx), py) if stage == 0 else (px, lax.rem(py + k, ny))
                remote(sum_out.at[step, stage], inbox.at[step, k - 1], send, recv, to).start()
                return carry

            lax.fori_loop(1, count, tell, 0)
            remote(inbox.at[step], inbox.at[step], send, recv, (right, upper)).wait_recv()
            value = value + jnp.sum(inbox[step], axis=0)
        for stage, count, inbox in ((0, nx, sum_x), (1, ny, sum_y)):
            send, recv = a_send.at[step, stage], a_recv.at[step, stage]
            remote(inbox.at[step], inbox.at[step], send, recv, (right, upper)).wait_send()
        return [value[:, n : n + 1] for n in range(len(values))]

    def inner(a, b):
        return jnp.sum(a * b, axis=1, keepdims=True)

    residual = load_row
    direction = residual
    mapped = product(0, residual)
    norm, energy = summed(0, [inner(residual, residual), inner(residual, mapped)])
    step_size = norm / energy
    solution_row = step_size * direction
    for step in range(1, ITERS):
        residual = residual - step_size * mapped
        send_vector(step, residual)
        image_row = product(step, residual)
        norm_next, plain, cross = summed(
            step,
            [
                inner(residual, residual),
                inner(residual, image_row),
                inner(residual, mapped) + inner(direction, image_row),
            ],
        )
        ratio = norm_next / norm
        energy = plain + ratio * cross + ratio * ratio * energy
        direction = residual + ratio * direction
        mapped = image_row + ratio * mapped
        norm = norm_next
        step_size = norm / energy
        solution_row = solution_row + step_size * direction
    answer[0] = solution_row


def body(deflation, layers, layer_table, forcing):
    nx = lax.axis_size("gx")
    ny = lax.axis_size("gy")
    weights = (
        unity_weights(lax.axis_index("gx"), nx, CX)[:, None]
        * unity_weights(lax.axis_index("gy"), ny, CY)[None, :]
        * (1.0 / math.sqrt(CX * CY * CZ))
    )
    basis = jnp.transpose(deflation, (1, 2, 0, 3)) * weights[:, :, None, None]
    vmem = pl.BlockSpec(memory_space=pltpu.VMEM)
    dma = pltpu.SemaphoreType.DMA
    rows, answer = pl.pallas_call(
        functools.partial(kernel, nx, ny),
        out_shape=(
            jax.ShapeDtypeStruct((9, VEC, VEC), F32),
            jax.ShapeDtypeStruct((1, 1, VEC), F32),
        ),
        in_specs=[vmem, vmem, pl.BlockSpec(memory_space=pltpu.SMEM), vmem],
        out_specs=(vmem, vmem),
        scratch_shapes=[
            pltpu.VMEM((12, 7, 2, CZ), F32),
            pltpu.VMEM((12, 7, VEC, CZ), F32),
            pltpu.VMEM((12, 7, VEC, CZ), F32),
            pltpu.VMEM((3, EY, VEC, CZ), F32),
            pltpu.VMEM((6, 3, VEC, CZ), F32),
            pltpu.VMEM((4, 3, VEC, CZ), F32),
            pltpu.VMEM((3, 3, VEC, CZ), F32),
            pltpu.VMEM((3, 3, VEC, CZ), F32),
            pltpu.VMEM((5, 8, CZ), F32),
            pltpu.VMEM((5, 8, CZ), F32),
            pltpu.VMEM((ITERS, 1, CZ), F32),
            pltpu.VMEM((ITERS, 8, 1, CZ), F32),
            pltpu.VMEM((ITERS, 2, 1, CZ), F32),
            pltpu.VMEM((ITERS, nx - 1, 1, CZ), F32),
            pltpu.VMEM((ITERS, ny - 1, 1, CZ), F32),
            dma((8,)), dma((8,)), dma((6,)), dma((6,)), dma((2,)), dma((2,)),
            dma((6,)), dma((6,)), dma((5,)), dma((5,)),
            dma((ITERS, 8)), dma((ITERS, 8)), dma((ITERS, 2)), dma((ITERS, 2)),
        ],
        compiler_params=pltpu.CompilerParams(
            collective_id=0, has_side_effects=True, vmem_limit_bytes=32 * 1024 * 1024
        ),
        name="coarse",
    )(basis, layers, layer_table, forcing)
    return rows[None, None], answer


def solution(mesh):
    return jax.shard_map(
        body,
        mesh=mesh,
        in_specs=(P(None, "gx", "gy", None), P("gx", "gy", None), P(), P("gx", "gy", None)),
        out_specs=(P("gx", "gy", None, None, None), P("gx", "gy", None)),
        check_vma=False,
    )
```

time: 2030 us -> 118 us (0.06)
  waiting for transfers between devices: 1890 us -> 0 us
  Pallas kernels: 0 us -> 113 us
  local copies, waits for them, and re-layouts: 39 us -> 2.47 us
  starting transfers between devices: 33.2 us -> 0 us
  other arithmetic: 33.9 us -> 1.37 us
    all_gather x1 -> x0, waiting for transfers between devices: 1420 us -> none  [body(): lax.all_gather(coarse_rows[4:].reshape(1, 5 * VEC * VEC), ('gx', 'gy'), a...]
    unnamed x3 -> x0, waiting for transfers between devices: 404 us -> none
    pallas_call x0 -> x1, Pallas kernels: none -> 113 us  [body(): pl.pallas_call(functools.partial(kernel, nx, ny), out_shape=(jax.ShapeDty...]
    ppermute x8 -> x0, waiting for transfers between devices: 71.6 us -> none  [the longest x4 49.9 us: extended(): after = lax.ppermute(initial, axis, down)]
    ppermute x8 -> x0, starting transfers between devices: 33.1 us -> none  [the longest x4 19.3 us: extended(): before = lax.ppermute(last, axis, up)]
    reduce_sum x11 -> x0, other arithmetic: 27.4 us -> none  [the longest x3 14.6 us: half_product(): result = result + jnp.sum(coarse_block * moved[None, :, :], axis=1)]
    all_gather x3 -> x0, local copies, waits for them, and re-layouts: 23 us -> none  [the longest x1 22 us: body(): lax.all_gather(coarse_rows[4:].reshape(1, 5 * VEC * VEC), ('gx', 'gy'), a...]
  transfers between devices with their start and end apart: 10 -> 0, of which waited for: 4 -> 0; matrix products, arithmetic and copies ran while one was open for 1% -> 0% of each run, Pallas kernels for 0% -> 0%
where the time goes in v1:
time: 118 us
  Pallas kernels  113 us (96%)
  local copies, waits for them, and re-layouts  2.47 us (2%)
  other arithmetic  1.37 us (1%)
    pallas_call x1, Pallas kernels, body(): pl.pallas_call(functools.partial(kernel, nx, ny), out_shape=(jax.ShapeDty...  113 us
    unnamed x10, local copies, waits for them, and re-layouts  2.47 us

profile of v1, /device:TPU:1, one launch (start us, length us, event | category | flops | bytes accessed | tf_op | source)
XLA Modules:
  0.0 118.0 jit_solution(15004440534843771467)
XLA Ops:
  0.6 0.0 copy-start.1
  0.7 0.1 multiply_multiply_fusion
  0.8 0.6 copy-done.1
  1.4 0.0 copy-start.2
  1.4 0.7 copy-done.2
  2.1 0.0 copy-start
  2.1 1.3 %multiply_bitcast_fusion.basis = f32[10,5,32,128]{3,2,1,0:T(8,128)S(1)} fusion(f32[32,10,5,128]{3,0,2,1:T(8,128)} %param.4, f32[10,5]{1,0:T(8,128)S(1)} %multiply_multiply_fusion), kind=kLoop, calls=%fused_computation | loop fusion | flops 204800 | bytes 1638600 | tf_op jit(solution)/shard_map/mul | solution.py:411
  3.4 0.0 copy-done
  3.4 113.5 %coarse.1 = (f32[9,32,32]{2,1,0:T(8,128)S(1)}, f32[1,1,32]{2,1,0:T(1,128)S(1)}) custom-call(f32[10,5,32,128]{3,2,1,0:T(8,128)S(1)} %multiply_bitcast_fusion.basis, s32[8,3,128]{2,1,0:T(4,128)S(1)} %copy.6.layers, f32[85]{0:T(128)S(1)} %copy-done, f32[8,3,128]{2,1,0:T(4,128)S(1)} %copy.7.forcing), custom_call_target="tpu_custom_call" | custom-call | tf_op jit(solution)/shard_map/coarse/pallas_call | solution.py:414
  116.8 0.7 copy.10
  117.5 0.5 copy.11
  (4 shorter events, 0.0 us)
Async XLA Ops:
  0.6 0.7 copy-start.1
  1.4 0.7 copy-start.2
  2.1 1.3 %copy-start = (f32[85]{0:T(128)S(1)}, f32[85]{0:T(128)}, u32[]{:S(2)}) copy-start(f32[85]{0:T(128)} %table.1) | copy-start | bytes 1024

commit v2 on v1

v2 whole, which is shorter than its diff:
```python
import functools
import math

import jax
import jax.numpy as jnp
from jax import lax
from jax.experimental import pallas as pl
from jax.experimental.pallas import tpu as pltpu
from jax.sharding import PartitionSpec as P

VEC = 32
CX = 8
CY = 3
CZ = 128
MARGIN = 1
LAYERS = 85
ITERS = 3
EX = 10
EY = 5
MESH = pl.DeviceIdType.MESH
F32 = jnp.float32
BF16 = jnp.bfloat16

EDGE = (0, 1, 2, 7, 8, 9)
DIRS = ((1, 0), (-1, 0), (0, 1), (0, -1), (1, 1), (-1, 1), (1, -1), (-1, -1))
SEND_X = {1: (8, 2), -1: (2, 2), 0: (2, 8)}
LAND_X = {1: (0, 2), -1: (10, 2), 0: (2, 8)}
SEND_Y = {1: (3, 2), -1: (2, 2), 0: (2, 3)}
LAND_Y = {1: (0, 2), -1: (5, 2), 0: (2, 3)}


HALO_X = {1: (7, 3, 0), -1: (0, 3, 9), 0: (0, 10, 1)}
HALO_Y = {1: (2, 3, 0), -1: (0, 3, 4), 0: (0, 5, 1)}
PAIRS = ((0, 0), (0, 1), (0, 2), (0, 3), (1, 1), (1, 2), (1, 3), (2, 2), (2, 3))
SHRINK = 0.125
QUIET = 1e-13


def sum_stages(nx, ny):
    low_x = 8 if nx % 8 == 0 else 2
    low_y = 4 if ny % 4 == 0 and ny > 4 else 2
    return (
        ((0, 1, low_x),),
        ((0, low_x, nx // low_x), (1, 1, low_y)),
        ((1, low_y, ny // low_y),),
    )


def members(digits):
    return math.prod(count for axis, stride, count in digits)


def two_sum(a, b):
    total = a + b
    back = total - a
    return total, (a - (total - back)) + (b - back)


def quick_sum(a, b):
    total = a + b
    return total, b - (total - a)


def halves(a):
    big = 4097.0 * a
    high = big - (big - a)
    return high, a - high


def two_product(a, b):
    product = a * b
    ah, al = halves(a)
    bh, bl = halves(b)
    return product, ((ah * bh - product) + ah * bl + al * bh) + al * bl


def add2(a, b):
    total, err = two_sum(a[0], b[0])
    return quick_sum(total, err + (a[1] + b[1]))


def mul2(a, b):
    product, err = two_product(a[0], b[0])
    return quick_sum(product, err + (a[0] * b[1] + a[1] * b[0]))


def neg2(a):
    return -a[0], -a[1]


def div2(a, b):
    first = a[0] / b[0]
    rest = add2(a, neg2(mul2(b, (first, jnp.zeros_like(first)))))
    return quick_sum(first, rest[0] / b[0])


def total2(terms):
    result = terms[0]
    for term in terms[1:]:
        result = add2(result, term)
    return result


def three_steps(gram):
    at = {}
    for (i, j), value in zip(PAIRS, gram):
        at[i, j] = at[j, i] = value
    one = (jnp.ones_like(gram[0][0]), jnp.zeros_like(gram[0][0]))
    residual, direction = [one], [one]
    solution = []
    norm = first = at[0, 0]
    for step in range(ITERS):
        size = len(direction)
        energy = total2(
            [
                mul2(mul2(direction[i], direction[j]), at[i, j + 1])
                for i in range(size)
                for j in range(size)
            ]
        )
        length = div2(norm, energy)
        if step > 0:
            live = norm[0] > QUIET * first[0]
            length = tuple(jnp.where(live, part, 0.0) for part in length)
        moved = [mul2(length, d) for d in direction]
        solution = [add2(x, m) for x, m in zip(solution, moved)] + moved[len(solution) :]
        if step == ITERS - 1:
            break
        back = [neg2(m) for m in moved]
        residual = [residual[0]] + [
            add2(residual[k], back[k - 1]) if k < len(residual) else back[k - 1]
            for k in range(1, size + 1)
        ]
        count = len(residual)
        terms = []
        for i in range(count):
            for j in range(i, count):
                term = mul2(mul2(residual[i], residual[j]), at[i, j])
                terms.append(term if i == j else (2.0 * term[0], 2.0 * term[1]))
        norm_next = total2(terms)
        ratio = div2(norm_next, norm)
        if step > 0:
            ratio = tuple(jnp.where(live, part, 0.0) for part in ratio)
        direction = [
            add2(residual[k], mul2(ratio, direction[k])) if k < size else residual[k]
            for k in range(count)
        ]
        norm = norm_next
    return [x[0] for x in solution]


def pack(cells):
    highs = [c.astype(BF16) for c in cells]
    lows = [(c - h.astype(F32)).astype(BF16) for c, h in zip(cells, highs)]
    high = jnp.concatenate(highs, axis=1)
    low = jnp.concatenate(lows, axis=1)
    return jnp.concatenate([high, low], axis=0)


def dot_cells(left, right):
    return lax.dot_general(
        pack(left), pack(right), (((1,), (1,)), ((), ())), preferred_element_type=F32
    )


def fold(wide):
    tall = wide[0:VEC] + wide[VEC:]
    return tall[:, 0:VEC] + tall[:, VEC:]


def squeeze_block(block):
    return jnp.concatenate([block[8 * g : 8 * g + 8] for g in range(4)], axis=1)


def spread_block(packed):
    return jnp.concatenate([packed[:, VEC * g : VEC * g + VEC] for g in range(4)], axis=0)


def kernel(
    nx, ny, raw_hbm, layers_hbm, table, forcing_hbm, rows, answer,
    basis, entry_in, force_in, field, weighted, image, diag, strip_x, strip_y, strip_m,
    corner_r, corner_l, block_out, block_in, spread_out, spread_in, whole, shaded, sum_out,
    l_sem, f_send, f_recv, y_send, y_recv, x_send, x_recv, m_send, m_recv, c_send, c_recv,
    b_send, b_recv, v_send, v_recv, a_send, a_recv, *sums,
):
    px = lax.axis_index("gx")
    py = lax.axis_index("gy")
    stages = sum_stages(nx, ny)
    loads = [
        pltpu.make_async_copy(src, dst, l_sem.at[n])
        for n, (src, dst) in enumerate(
            ((layers_hbm, entry_in), (forcing_hbm, force_in), (raw_hbm, basis))
        )
    ]
    for load_copy in loads:
        load_copy.start()
    right, left = lax.rem(px + 1, nx), lax.rem(px + nx - 1, nx)
    upper, lower = lax.rem(py + 1, ny), lax.rem(py + ny - 1, ny)
    at_x = {1: right, -1: left, 0: px}
    at_y = {1: upper, -1: lower, 0: py}
    has_right, has_left = px < nx - 1, px > 0
    has_up, has_down = py < ny - 1, py > 0

    def remote(src, dst, send, recv, to):
        return pltpu.make_async_remote_copy(
            src_ref=src, dst_ref=dst, send_sem=send, recv_sem=recv, device_id=to, device_id_type=MESH
        )

    barrier = pltpu.get_barrier_semaphore()

    def partner(digits, k):
        place = [px, py]
        for axis, stride, count in digits:
            step, k = k % count, k // count
            digit = lax.rem(lax.div(place[axis], stride), count)
            place[axis] = place[axis] + (lax.rem(digit + step, count) - digit) * stride
        return tuple(place)

    for dx, dy in DIRS:
        pl.semaphore_signal(barrier, inc=1, device_id=(at_x[dx], at_y[dy]), device_id_type=MESH)
    for digits in stages:
        for k in range(1, members(digits)):
            pl.semaphore_signal(barrier, inc=1, device_id=partner(digits, k), device_id_type=MESH)

    loads[0].wait()
    entry = entry_in[...]

    def look_up(t, root):
        for k in range(5):
            root = jnp.where(entry == 5 * t + k, table[5 * t + k], root)
        return root

    root = jnp.sqrt(lax.fori_loop(0, LAYERS // 5, look_up, jnp.zeros((CY, CX, CZ), F32)))
    loads[1].wait()
    for x in range(CX):
        for y in range(CY):
            field[2 + x, 2 + y, 0:1, :] = root[y, x : x + 1, :]
            field[2 + x, 2 + y, 1:2, :] = force_in[y, x : x + 1, :]

    def weights_of(cells, has_below, has_above):
        low, high = jnp.where(has_below, 0.5, 1.0), jnp.where(has_above, 0.5, 1.0)
        low_end, high_end = jnp.where(has_below, 0.5, 0.0), jnp.where(has_above, 0.5, 0.0)
        return [low_end, low] + [1.0] * (cells - 4) + [high, high_end]

    scale_x = [w * (1.0 / math.sqrt(CX * CY * CZ)) for w in weights_of(EX, has_left, has_right)]
    scale_y = weights_of(EY, has_down, has_up)
    loads[2].wait()
    for ex in range(EX):
        for ey in range(EY):
            basis[ex, ey] = basis[ex, ey] * (scale_x[ex] * scale_y[ey])

    pl.semaphore_wait(barrier, 8 + sum(members(d) - 1 for d in stages))

    field_copies = []
    for n, (dx, dy) in enumerate(DIRS):
        sx, lx = SEND_X[dx]
        sy, ly = SEND_Y[dy]
        tx = LAND_X[dx][0]
        ty = LAND_Y[dy][0]
        field_copies.append(
            remote(
                field.at[pl.ds(sx, lx), pl.ds(sy, ly)],
                field.at[pl.ds(tx, lx), pl.ds(ty, ly)],
                f_send.at[n], f_recv.at[n], (at_x[dx], at_y[dy]),
            )
        )
        field_copies[-1].start()
    strip_copies = [
        remote(
            basis.at[ex, pl.ds(0, 3)], strip_y.at[n], y_send.at[n], y_recv.at[n], (px, lower)
        )
        for n, ex in enumerate(EDGE)
    ]
    strip_copies[0].start()
    x_copy = remote(basis.at[pl.ds(0, 3)], strip_x, x_send, x_recv, (left, py))
    x_copy.start()

    empty = jnp.zeros((VEC, CZ), F32)
    for j in range(7):
        weighted[0, j] = empty
        weighted[11, j] = empty

    def zero_rows(i, carry):
        weighted[i, 0] = empty
        weighted[i, 6] = empty
        return carry

    lax.fori_loop(1, 11, zero_rows, 0)

    for copy in field_copies:
        copy.wait()

    @pl.when(px == 0)
    def _():
        field[0:2] = jnp.zeros((2, 7, 2, CZ), F32)

    @pl.when(px == nx - 1)
    def _():
        field[10:12] = jnp.zeros((2, 7, 2, CZ), F32)

    @pl.when(py == 0)
    def _():
        field[:, 0:2] = jnp.zeros((12, 2, 2, CZ), F32)

    @pl.when(py == ny - 1)
    def _():
        field[:, 5:7] = jnp.zeros((12, 2, 2, CZ), F32)

    lane1 = lax.broadcasted_iota(jnp.int32, (1, CZ), 1)
    lane32 = lax.broadcasted_iota(jnp.int32, (VEC, CZ), 1)

    def beside(value, lane):
        before = jnp.where(lane > 0, pltpu.roll(value, 1, 1), 0.0)
        after = jnp.where(lane < CZ - 1, pltpu.roll(value, CZ - 1, 1), 0.0)
        return before + after

    def scale(i, load):
        for j in range(1, 6):
            value = basis[i - 1, j - 1]
            own = field[i, j, 0:1, :]
            weighted[i, j] = own * value
            load = load + field[i, j, 1:2, :] * value
            near = (
                field[i - 1, j, 0:1, :] + field[i + 1, j, 0:1, :]
                + field[i, j - 1, 0:1, :] + field[i, j + 1, 0:1, :] + beside(own, lane1)
            )
            diag[i, j] = 0.5 + own * near
        return load

    load = lax.fori_loop(1, 11, scale, empty)

    row_id = lax.broadcasted_iota(jnp.int32, (VEC, VEC), 0)
    col_id = lax.broadcasted_iota(jnp.int32, (VEC, VEC), 1)
    diagonal = row_id == col_id

    def as_row(column):
        return jnp.sum(jnp.where(diagonal, column, 0.0), axis=0, keepdims=True)

    def halo_copies(step):
        result = []
        for n, (dx, dy) in enumerate(DIRS):
            sx, lx, unused = HALO_X[dx]
            sy, ly, unused = HALO_Y[dy]
            result.append(
                remote(
                    spread_out.at[step, pl.ds(sx, lx), pl.ds(sy, ly)],
                    spread_in.at[step, n, pl.ds(0, lx), pl.ds(0, ly)],
                    v_send.at[step, n], v_recv.at[step, n], (at_x[dx], at_y[dy]),
                )
            )
        return result

    halos = [halo_copies(step) for step in range(ITERS)]

    def send_spread(step, column):
        def spread(ex, carry):
            for ey in range(EY):
                spread_out[step, ex, ey] = jnp.sum(basis[ex, ey] * column, axis=0, keepdims=True)
            return carry

        lax.fori_loop(0, EX, spread, 0)
        for copy in halos[step]:
            copy.start()

    exists = {(1, 0): has_left, (-1, 0): has_right, (0, 1): has_down, (0, -1): has_up}

    def gather_back(step):
        whole[...] = jnp.zeros((12, 7, 1, CZ), F32)
        whole[1:11, 1:6] = spread_out[step]
        for n, (dx, dy) in enumerate(DIRS):
            halos[step][n].wait()
            lx, tx = HALO_X[dx][1:]
            ly, ty = HALO_Y[dy][1:]
            there = exists[dx, 0] if dy == 0 else exists[0, dy] if dx == 0 else exists[dx, 0] & exists[0, dy]
            piece = jnp.where(there, spread_in[step, n, 0:lx, 0:ly], 0.0)
            whole[tx : tx + lx, ty : ty + ly] = whole[tx : tx + lx, ty : ty + ly] + piece

        def shade(i, carry):
            for j in range(7):
                shaded[i, j] = field[i, j, 0:1, :] * whole[i, j]
            return carry

        lax.fori_loop(0, 12, shade, 0)

        def collect(i, total):
            for j in range(1, 6):
                near = (
                    shaded[i - 1, j] + shaded[i + 1, j] + shaded[i, j - 1] + shaded[i, j + 1]
                    + beside(shaded[i, j], lane1)
                )
                value = diag[i, j] * whole[i, j] - field[i, j, 0:1, :] * near
                total = total + basis[i - 1, j - 1] * value
            return total

        return jnp.sum(lax.fori_loop(1, 11, collect, empty), axis=1, keepdims=True) * SHRINK

    columns = [jnp.sum(load, axis=1, keepdims=True)]
    send_spread(0, columns[0])
    strip_copies[5].start()

    def image_inside(i, j):
        total = (
            weighted[i - 1, j] + weighted[i + 1, j] + weighted[i, j - 1] + weighted[i, j + 1]
            + beside(weighted[i, j], lane32)
        )
        image[i, j] = diag[i, j] * basis[i - 1, j - 1] - field[i, j, 0:1, :] * total

    def image_above(i):
        image[i, 6] = -(field[i, 6, 0:1, :] * weighted[i, 5])

    def upper_rows(i, carry):
        image_inside(i, 4)
        image_inside(i, 5)
        image_above(i)
        return carry

    def lower_rows(i, carry):
        for j in (1, 2, 3):
            image_inside(i, j)
        return carry

    lax.fori_loop(4, 8, upper_rows, 0)
    m_copies = [
        remote(image.at[4 + k, pl.ds(4, 3)], strip_m.at[k], m_send.at[k], m_recv.at[k], (px, upper))
        for k in range(4)
    ]
    m_copies[0].start()
    lax.fori_loop(1, 4, upper_rows, 0)
    lax.fori_loop(8, 11, upper_rows, 0)
    lax.fori_loop(1, 11, lower_rows, 0)
    for j in (4, 5):
        image[0, j] = -(field[0, j, 0:1, :] * weighted[1, j])
    image[0, 6] = empty
    image[11, 6] = empty
    for j in range(1, 6):
        image[11, j] = -(field[11, j, 0:1, :] * weighted[10, j])

    columns.append(gather_back(0))
    send_spread(1, columns[1])
    for copy in (strip_copies[1], m_copies[1], strip_copies[4], m_copies[2]):
        copy.start()

    def own_block(t, total):
        i = 1 + 2 * t
        cells = [(i + k, j) for k in (0, 1) for j in range(1, 6)]
        return total + dot_cells(
            [image[a, b] for a, b in cells], [basis[a - 1, b - 1] for a, b in cells]
        )

    rows[4] = fold(lax.fori_loop(0, 5, own_block, jnp.zeros((2 * VEC, 2 * VEC), F32)))

    def send_block(n, block, to):
        block_out[n] = squeeze_block(block)
        copy = remote(block_out.at[n], block_in.at[n], b_send.at[n], b_recv.at[n], to)
        copy.start()
        return copy

    columns.append(gather_back(1))
    send_spread(2, columns[2])
    for copy in (strip_copies[2], m_copies[3], strip_copies[3]):
        copy.start()

    x_copy.wait()
    block_x = fold(
        dot_cells(
            [image[9 + k, 1 + j] for k in range(3) for j in range(EY)],
            [strip_x[k, j] for k in range(3) for j in range(EY)],
        )
    )
    rows[7] = jnp.where(has_right, block_x, 0.0)
    block_copies = [send_block(0, block_x.T, (right, py))]

    corner_copies = {}

    def hand_on(n):
        strip_copies[n].wait()
        if n < 3:
            copy = remote(strip_y.at[n], corner_r.at[n], c_send.at[n], c_recv.at[n], (left, py))
        else:
            copy = remote(strip_y.at[n], corner_l.at[n - 3], c_send.at[n], c_recv.at[n], (right, py))
        copy.start()
        corner_copies[n] = copy

    hand_on(0)
    hand_on(5)
    columns.append(gather_back(2))

    blank = jnp.zeros((1, CZ - VEC), F32)
    vectors = [jnp.concatenate([as_row(c), blank], axis=1) for c in columns]
    slot = lax.broadcasted_iota(jnp.int32, (16, CZ), 0)
    lane16 = lax.broadcasted_iota(jnp.int32, (16, CZ), 1)
    one_side = other_side = jnp.zeros((16, CZ), F32)
    for n, (i, j) in enumerate(PAIRS):
        one_side = jnp.where(slot == n, vectors[i], one_side)
        other_side = jnp.where(slot == n, vectors[j], other_side)
    gram = two_product(one_side, other_side)
    for shift in (16, 8, 4, 2, 1):
        gram = add2(gram, tuple(pltpu.roll(part, CZ - shift, 1) for part in gram))
    value = tuple(
        jnp.sum(jnp.where(slot == lane16, part[:, 0:1], 0.0), axis=0, keepdims=True)
        for part in gram
    )

    sum_copies = []

    def tell(stage):
        sum_out[stage] = jnp.concatenate(value, axis=0)
        for k in range(1, members(stages[stage])):
            remote(
                sum_out.at[stage], sums[stage].at[k - 1],
                a_send.at[stage], a_recv.at[stage], partner(stages[stage], k),
            ).start()

    def hear(stage):
        whole_inbox = remote(
            sums[stage], sums[stage], a_send.at[stage], a_recv.at[stage], (right, upper)
        )
        whole_inbox.wait()
        result = value
        for k in range(1, members(stages[stage])):
            message = sums[stage][k - 1]
            result = add2(result, (message[0:1], message[1:2]))
        return result

    tell(0)
    hand_on(1)
    hand_on(4)
    value = hear(0)
    tell(1)
    for copy in m_copies:
        copy.wait()
    part_m = fold(
        dot_cells(
            [strip_m[k, j] for k in range(4) for j in range(3)],
            [basis[3 + k, j] for k in range(4) for j in range(3)],
        )
    )
    block_copies.append(send_block(1, part_m, (px, lower)))
    hand_on(2)
    hand_on(3)
    part_e = fold(
        dot_cells(
            [image[1 + k, 4 + j] for k in range(3) for j in range(3)],
            [strip_y[k, j] for k in range(3) for j in range(3)],
        )
        + dot_cells(
            [image[8 + k, 4 + j] for k in range(3) for j in range(3)],
            [strip_y[3 + k, j] for k in range(3) for j in range(3)],
        )
    )
    block_copies.append(send_block(2, part_e.T, (px, upper)))
    value = hear(1)
    tell(2)
    for n in range(3):
        corner_copies[n].wait()
    block_r = fold(
        dot_cells(
            [image[9 + k, 4 + j] for k in range(3) for j in range(3)],
            [corner_r[k, j] for k in range(3) for j in range(3)],
        )
    )
    block_copies.append(send_block(3, block_r.T, (right, upper)))
    for n in range(3, 6):
        corner_copies[n].wait()
    block_l = fold(
        dot_cells(
            [image[k, 4 + j] for k in range(3) for j in range(3)],
            [corner_l[k, j] for k in range(3) for j in range(3)],
        )
    )
    block_copies.append(send_block(4, block_l.T, (left, upper)))
    value = hear(2)
    steps = three_steps([tuple(part[:, n : n + 1] for part in value) for n in range(len(PAIRS))])
    found = SHRINK * (steps[0] * vectors[0] + steps[1] * vectors[1] + steps[2] * vectors[2])
    answer[0] = found[:, 0:VEC]

    rows[8] = jnp.where(has_right & has_up, block_r, 0.0)
    rows[2] = jnp.where(has_left & has_up, block_l, 0.0)
    for copy in block_copies:
        copy.wait()
    rows[1] = jnp.where(has_left, spread_block(block_in[0]), 0.0)
    rows[5] = jnp.where(has_up, part_e + spread_block(block_in[1]), 0.0)
    rows[3] = jnp.where(has_down, part_m.T + spread_block(block_in[2]), 0.0)
    rows[0] = jnp.where(has_left & has_down, spread_block(block_in[3]), 0.0)
    rows[6] = jnp.where(has_right & has_down, spread_block(block_in[4]), 0.0)


def body(deflation, layers, layer_table, forcing):
    nx = lax.axis_size("gx")
    ny = lax.axis_size("gy")
    vmem = pl.BlockSpec(memory_space=pltpu.VMEM)
    hbm = pl.BlockSpec(memory_space=pltpu.HBM)
    dma = pltpu.SemaphoreType.DMA
    stages = sum_stages(nx, ny)
    rows, answer = pl.pallas_call(
        functools.partial(kernel, nx, ny),
        out_shape=(
            jax.ShapeDtypeStruct((9, VEC, VEC), F32),
            jax.ShapeDtypeStruct((1, 1, VEC), F32),
        ),
        in_specs=[hbm, hbm, pl.BlockSpec(memory_space=pltpu.SMEM), hbm],
        out_specs=(vmem, vmem),
        scratch_shapes=[
            pltpu.VMEM((EX, EY, VEC, CZ), F32),
            pltpu.VMEM((CY, CX, CZ), jnp.int32),
            pltpu.VMEM((CY, CX, CZ), F32),
            pltpu.VMEM((12, 7, 2, CZ), F32),
            pltpu.VMEM((12, 7, VEC, CZ), F32),
            pltpu.VMEM((12, 7, VEC, CZ), F32),
            pltpu.VMEM((12, 7, 1, CZ), F32),
            pltpu.VMEM((3, EY, VEC, CZ), F32),
            pltpu.VMEM((6, 3, VEC, CZ), F32),
            pltpu.VMEM((4, 3, VEC, CZ), F32),
            pltpu.VMEM((3, 3, VEC, CZ), F32),
            pltpu.VMEM((3, 3, VEC, CZ), F32),
            pltpu.VMEM((5, 8, CZ), F32),
            pltpu.VMEM((5, 8, CZ), F32),
            pltpu.VMEM((ITERS, EX, EY, 1, CZ), F32),
            pltpu.VMEM((ITERS, 8, EX, EY, 1, CZ), F32),
            pltpu.VMEM((12, 7, 1, CZ), F32),
            pltpu.VMEM((12, 7, 1, CZ), F32),
            pltpu.VMEM((len(stages), 2, CZ), F32),
            dma((3,)), dma((8,)), dma((8,)), dma((6,)), dma((6,)), dma, dma,
            dma((4,)), dma((4,)), dma((6,)), dma((6,)), dma((5,)), dma((5,)),
            dma((ITERS, 8)), dma((ITERS, 8)), dma((len(stages),)), dma((len(stages),)),
            *[pltpu.VMEM((members(digits) - 1, 2, CZ), F32) for digits in stages],
        ],
        compiler_params=pltpu.CompilerParams(
            collective_id=0, has_side_effects=True, vmem_limit_bytes=32 * 1024 * 1024
        ),
        name="coarse",
    )(
        jnp.transpose(deflation, (1, 2, 0, 3)),
        jnp.transpose(layers, (1, 0, 2)),
        layer_table,
        jnp.transpose(forcing, (1, 0, 2)),
    )
    return rows[None, None], answer


def solution(mesh):
    return jax.shard_map(
        body,
        mesh=mesh,
        in_specs=(P(None, "gx", "gy", None), P("gx", "gy", None), P(), P("gx", "gy", None)),
        out_specs=(P("gx", "gy", None, None, None), P("gx", "gy", None)),
        check_vma=False,
    )
```

time: 118 us -> 86.4 us (0.73)
  Pallas kernels: 113 us -> 81.1 us
  local copies, waits for them, and re-layouts: 2.47 us -> 4.38 us
  other arithmetic: 1.37 us -> 0 us
    pallas_call x1, Pallas kernels: 113 us -> 81.1 us  [body(): pl.pallas_call(functools.partial(kernel, nx, ny), out_shape=(jax.ShapeDty...]
    unnamed x10, local copies, waits for them, and re-layouts: 2.47 us -> 4.38 us
    mul x2 -> x0, other arithmetic: 1.35 us -> none  [the longest x1 1.27 us: body(): basis = jnp.transpose(deflation, (1, 2, 0, 3)) * weights[:, :, None, None]]
where the time goes in v2:
time: 86.4 us; the launch traced here: 86.1 us
  Pallas kernels  81.1 us (94%)
  local copies, waits for them, and re-layouts  4.38 us (5%)
    pallas_call x1, Pallas kernels, body(): pl.pallas_call(functools.partial(kernel, nx, ny), out_shape=(jax.ShapeDty...  81.1 us
    unnamed x10, local copies, waits for them, and re-layouts  4.38 us

profile of v2, /device:TPU:1, one launch (start us, length us, event | category | flops | bytes accessed | tf_op | source)
XLA Modules:
  0.0 86.1 jit_solution(12798984808373607584)
XLA Ops:
  0.6 0.0 copy-start.3
  0.6 0.6 copy-done.3
  1.3 0.0 copy-start
  1.3 1.1 %copy-done = f32[32,10,5,128]{3,0,2,1:T(8,128)S(1)} copy-done((f32[32,10,5,128]{3,0,2,1:T(8,128)S(1)}, f32[32,10,5,128]{3,0,2,1:T(8,128)}, u32[]{:S(2)}) %copy-start) | copy-done | bytes 819224
  2.4 0.0 copy-start.1
  2.4 0.7 copy-done.1
  3.1 0.0 copy-start.2
  3.1 0.7 copy-done.2
  3.8 81.1 %coarse.1 = (f32[9,32,32]{2,1,0:T(8,128)S(1)}, f32[1,1,32]{2,1,0:T(1,128)S(1)}) custom-call(f32[10,5,32,128]{3,2,1,0:T(8,128)S(1)} %bitcast.4, s32[3,8,128]{2,1,0:T(8,128)S(1)} %bitcast.6, f32[85]{0:T(128)S(1)} %copy-done.3, f32[3,8,128]{2,1,0:T(8,128)S(1)} %bitcast.7), custom_call_target="tpu_custom_call" | custom-call | tf_op jit(solution)/shard_map/coarse/pallas_call | solution.py:595
  84.9 0.7 copy.8
  85.6 0.5 copy.9
Async XLA Ops:
  0.6 0.7 copy-start.3
  1.3 1.1 %copy-start = (f32[32,10,5,128]{3,0,2,1:T(8,128)S(1)}, f32[32,10,5,128]{3,0,2,1:T(8,128)}, u32[]{:S(2)}) copy-start(f32[32,10,5,128]{3,0,2,1:T(8,128)} %param.4) | copy-start | bytes 2457604
  2.4 0.7 copy-start.1
  3.1 0.7 copy-start.2

commit v3 on v2

--- a/solution.py
+++ b/solution.py
@@ -22,7 +22,11 @@
 BF16 = jnp.bfloat16
 
 EDGE = (0, 1, 2, 7, 8, 9)
-DIRS = ((1, 0), (-1, 0), (0, 1), (0, -1), (1, 1), (-1, 1), (1, -1), (-1, -1))
+DIRS = ((0, 1), (0, -1), (1, 1), (-1, 1), (1, -1), (-1, -1), (1, 0), (-1, 0))
+UP = tuple((n, r) for n in (0, 5, 1, 4) for r in range(3)) + ((2, 0), (2, 1), (3, 0), (3, 1))
+DOWN = tuple((c, r) for c in (3, 4, 5, 6) for r in range(3)) + ((2, 2), (7, 2))
+UP_SHARE = (0, 4, 4, 4, 4)
+DOWN_SHARE = (0, 4, 3, 3, 4)
 SEND_X = {1: (8, 2), -1: (2, 2), 0: (2, 8)}
 LAND_X = {1: (0, 2), -1: (10, 2), 0: (2, 8)}
 SEND_Y = {1: (3, 2), -1: (2, 2), 0: (2, 3)}
@@ -265,13 +269,24 @@
             )
         )
         field_copies[-1].start()
-    strip_copies = [
-        remote(
-            basis.at[ex, pl.ds(0, 3)], strip_y.at[n], y_send.at[n], y_recv.at[n], (px, lower)
-        )
-        for n, ex in enumerate(EDGE)
+    up_copies = [
+        remote(basis.at[EDGE[n], r], strip_y.at[n, r], y_send.at[t], y_recv.at[t], (px, lower))
+        for t, (n, r) in enumerate(UP)
     ]
-    strip_copies[0].start()
+    down_copies = [
+        remote(image.at[c + 1, 4 + r], strip_m.at[t], m_send.at[t], m_recv.at[t], (px, upper))
+        for t, (c, r) in enumerate(DOWN)
+    ]
+
+    def feed(gap):
+        ups = up_copies[sum(UP_SHARE[:gap]) : sum(UP_SHARE[: gap + 1])]
+        downs = down_copies[sum(DOWN_SHARE[:gap]) : sum(DOWN_SHARE[: gap + 1])]
+        for t in range(max(len(ups), len(downs))):
+            for copies in (ups, downs):
+                if t < len(copies):
+                    copies[t].start()
+
+    feed(0)
     x_copy = remote(basis.at[pl.ds(0, 3)], strip_x, x_send, x_recv, (left, py))
     x_copy.start()
 
@@ -327,7 +342,7 @@
             diag[i, j] = 0.5 + own * near
         return load
 
-    load = lax.fori_loop(1, 11, scale, empty)
+    load = lax.fori_loop(1, 11, scale, empty, unroll=5)
 
     row_id = lax.broadcasted_iota(jnp.int32, (VEC, VEC), 0)
     col_id = lax.broadcasted_iota(jnp.int32, (VEC, VEC), 1)
@@ -358,7 +373,7 @@
                 spread_out[step, ex, ey] = jnp.sum(basis[ex, ey] * column, axis=0, keepdims=True)
             return carry
 
-        lax.fori_loop(0, EX, spread, 0)
+        lax.fori_loop(0, EX, spread, 0, unroll=True)
         for copy in halos[step]:
             copy.start()
 
@@ -380,7 +395,7 @@
                 shaded[i, j] = field[i, j, 0:1, :] * whole[i, j]
             return carry
 
-        lax.fori_loop(0, 12, shade, 0)
+        lax.fori_loop(0, 12, shade, 0, unroll=True)
 
         def collect(i, total):
             for j in range(1, 6):
@@ -392,11 +407,10 @@
                 total = total + basis[i - 1, j - 1] * value
             return total
 
-        return jnp.sum(lax.fori_loop(1, 11, collect, empty), axis=1, keepdims=True) * SHRINK
+        return jnp.sum(lax.fori_loop(1, 11, collect, empty, unroll=True), axis=1, keepdims=True) * SHRINK
 
     columns = [jnp.sum(load, axis=1, keepdims=True)]
     send_spread(0, columns[0])
-    strip_copies[5].start()
 
     def image_inside(i, j):
         total = (
@@ -420,25 +434,17 @@
         return carry
 
     lax.fori_loop(4, 8, upper_rows, 0)
-    m_copies = [
-        remote(image.at[4 + k, pl.ds(4, 3)], strip_m.at[k], m_send.at[k], m_recv.at[k], (px, upper))
-        for k in range(4)
-    ]
-    m_copies[0].start()
     lax.fori_loop(1, 4, upper_rows, 0)
     lax.fori_loop(8, 11, upper_rows, 0)
     lax.fori_loop(1, 11, lower_rows, 0)
     for j in (4, 5):
         image[0, j] = -(field[0, j, 0:1, :] * weighted[1, j])
-    image[0, 6] = empty
-    image[11, 6] = empty
     for j in range(1, 6):
         image[11, j] = -(field[11, j, 0:1, :] * weighted[10, j])
+    feed(1)
 
     columns.append(gather_back(0))
     send_spread(1, columns[1])
-    for copy in (strip_copies[1], m_copies[1], strip_copies[4], m_copies[2]):
-        copy.start()
 
     def own_block(t, total):
         i = 1 + 2 * t
@@ -448,6 +454,7 @@
         )
 
     rows[4] = fold(lax.fori_loop(0, 5, own_block, jnp.zeros((2 * VEC, 2 * VEC), F32)))
+    feed(2)
 
     def send_block(n, block, to):
         block_out[n] = squeeze_block(block)
@@ -457,8 +464,6 @@
 
     columns.append(gather_back(1))
     send_spread(2, columns[2])
-    for copy in (strip_copies[2], m_copies[3], strip_copies[3]):
-        copy.start()
 
     x_copy.wait()
     block_x = fold(
@@ -469,15 +474,17 @@
     )
     rows[7] = jnp.where(has_right, block_x, 0.0)
     block_copies = [send_block(0, block_x.T, (right, py))]
+    feed(3)
 
     corner_copies = {}
 
     def hand_on(n):
-        strip_copies[n].wait()
-        if n < 3:
-            copy = remote(strip_y.at[n], corner_r.at[n], c_send.at[n], c_recv.at[n], (left, py))
-        else:
-            copy = remote(strip_y.at[n], corner_l.at[n - 3], c_send.at[n], c_recv.at[n], (right, py))
+        for t in range(len(UP)):
+            if UP[t][0] == n:
+                up_copies[t].wait()
+        part = pl.ds(0, 2 if n in (2, 3) else 3)
+        inbox, to = (corner_r.at[n], left) if n < 3 else (corner_l.at[n - 3], right)
+        copy = remote(strip_y.at[n, part], inbox.at[part], c_send.at[n], c_recv.at[n], (to, py))
         copy.start()
         corner_copies[n] = copy
 
@@ -523,40 +530,31 @@
         return result
 
     tell(0)
+    feed(4)
     hand_on(1)
     hand_on(4)
     value = hear(0)
     tell(1)
-    for copy in m_copies:
+    for copy in down_copies:
         copy.wait()
     part_m = fold(
-        dot_cells(
-            [strip_m[k, j] for k in range(4) for j in range(3)],
-            [basis[3 + k, j] for k in range(4) for j in range(3)],
-        )
+        dot_cells([strip_m[t] for t in range(len(DOWN))], [basis[c, r] for c, r in DOWN])
     )
     block_copies.append(send_block(1, part_m, (px, lower)))
     hand_on(2)
     hand_on(3)
     part_e = fold(
         dot_cells(
-            [image[1 + k, 4 + j] for k in range(3) for j in range(3)],
-            [strip_y[k, j] for k in range(3) for j in range(3)],
-        )
-        + dot_cells(
-            [image[8 + k, 4 + j] for k in range(3) for j in range(3)],
-            [strip_y[3 + k, j] for k in range(3) for j in range(3)],
+            [image[EDGE[n] + 1, 4 + r] for n, r in UP], [strip_y[n, r] for n, r in UP]
         )
     )
     block_copies.append(send_block(2, part_e.T, (px, upper)))
-    value = hear(1)
-    tell(2)
     for n in range(3):
         corner_copies[n].wait()
     block_r = fold(
         dot_cells(
-            [image[9 + k, 4 + j] for k in range(3) for j in range(3)],
-            [corner_r[k, j] for k in range(3) for j in range(3)],
+            [image[9 + n, 4 + r] for n, r in UP if n < 3],
+            [corner_r[n, r] for n, r in UP if n < 3],
         )
     )
     block_copies.append(send_block(3, block_r.T, (right, upper)))
@@ -564,11 +562,13 @@
         corner_copies[n].wait()
     block_l = fold(
         dot_cells(
-            [image[k, 4 + j] for k in range(3) for j in range(3)],
-            [corner_l[k, j] for k in range(3) for j in range(3)],
+            [image[n - 3, 4 + r] for n, r in UP if n > 2],
+            [corner_l[n - 3, r] for n, r in UP if n > 2],
         )
     )
     block_copies.append(send_block(4, block_l.T, (left, upper)))
+    value = hear(1)
+    tell(2)
     value = hear(2)
     steps = three_steps([tuple(part[:, n : n + 1] for part in value) for n in range(len(PAIRS))])
     found = SHRINK * (steps[0] * vectors[0] + steps[1] * vectors[1] + steps[2] * vectors[2])
@@ -610,7 +610,7 @@
             pltpu.VMEM((12, 7, 1, CZ), F32),
             pltpu.VMEM((3, EY, VEC, CZ), F32),
             pltpu.VMEM((6, 3, VEC, CZ), F32),
-            pltpu.VMEM((4, 3, VEC, CZ), F32),
+            pltpu.VMEM((len(DOWN), VEC, CZ), F32),
             pltpu.VMEM((3, 3, VEC, CZ), F32),
             pltpu.VMEM((3, 3, VEC, CZ), F32),
             pltpu.VMEM((5, 8, CZ), F32),
@@ -620,8 +620,8 @@
             pltpu.VMEM((12, 7, 1, CZ), F32),
             pltpu.VMEM((12, 7, 1, CZ), F32),
             pltpu.VMEM((len(stages), 2, CZ), F32),
-            dma((3,)), dma((8,)), dma((8,)), dma((6,)), dma((6,)), dma, dma,
-            dma((4,)), dma((4,)), dma((6,)), dma((6,)), dma((5,)), dma((5,)),
+            dma((3,)), dma((8,)), dma((8,)), dma((16,)), dma((16,)), dma, dma,
+            dma((14,)), dma((14,)), dma((6,)), dma((6,)), dma((5,)), dma((5,)),
             dma((ITERS, 8)), dma((ITERS, 8)), dma((len(stages),)), dma((len(stages),)),
             *[pltpu.VMEM((members(digits) - 1, 2, CZ), F32) for digits in stages],
         ],

time: 86.4 us -> 76.2 us (0.88)
  Pallas kernels: 81.1 us -> 70.9 us
    pallas_call x1, Pallas kernels: 81.1 us -> 70.9 us  [body(): pl.pallas_call(functools.partial(kernel, nx, ny), out_shape=(jax.ShapeDty...]
where the time goes in v3:
time: 76.2 us; the launch traced here: 76 us
  Pallas kernels  70.9 us (93%)
  local copies, waits for them, and re-layouts  4.38 us (6%)
    pallas_call x1, Pallas kernels, body(): pl.pallas_call(functools.partial(kernel, nx, ny), out_shape=(jax.ShapeDty...  70.9 us
    unnamed x10, local copies, waits for them, and re-layouts  4.38 us

profile of v3, /device:TPU:1, one launch (start us, length us, event | category | flops | bytes accessed | tf_op | source)
XLA Modules:
  0.0 76.0 jit_solution(17597800751215979095)
XLA Ops:
  0.6 0.0 copy-start.3
  0.6 0.6 copy-done.3
  1.3 0.0 copy-start
  1.3 1.1 %copy-done = f32[32,10,5,128]{3,0,2,1:T(8,128)S(1)} copy-done((f32[32,10,5,128]{3,0,2,1:T(8,128)S(1)}, f32[32,10,5,128]{3,0,2,1:T(8,128)}, u32[]{:S(2)}) %copy-start) | copy-done | bytes 819224
  2.4 0.0 copy-start.1
  2.4 0.7 copy-done.1
  3.1 0.0 copy-start.2
  3.1 0.7 copy-done.2
  3.8 70.9 %coarse.1 = (f32[9,32,32]{2,1,0:T(8,128)S(1)}, f32[1,1,32]{2,1,0:T(1,128)S(1)}) custom-call(f32[10,5,32,128]{3,2,1,0:T(8,128)S(1)} %bitcast.4, s32[3,8,128]{2,1,0:T(8,128)S(1)} %bitcast.6, f32[85]{0:T(128)S(1)} %copy-done.3, f32[3,8,128]{2,1,0:T(8,128)S(1)} %bitcast.7), custom_call_target="tpu_custom_call" | custom-call | tf_op jit(solution)/shard_map/coarse/pallas_call | solution.py:595
  74.8 0.7 copy.8
  75.5 0.5 copy.9
Async XLA Ops:
  0.6 0.7 copy-start.3
  1.3 1.1 %copy-start = (f32[32,10,5,128]{3,0,2,1:T(8,128)S(1)}, f32[32,10,5,128]{3,0,2,1:T(8,128)}, u32[]{:S(2)}) copy-start(f32[32,10,5,128]{3,0,2,1:T(8,128)} %param.4) | copy-start | bytes 2457604
  2.4 0.7 copy-start.1
  3.1 0.7 copy-start.2

commit v4 on v3

--- a/solution.py
+++ b/solution.py
@@ -220,8 +220,57 @@
             place[axis] = place[axis] + (lax.rem(digit + step, count) - digit) * stride
         return tuple(place)
 
-    for dx, dy in DIRS:
-        pl.semaphore_signal(barrier, inc=1, device_id=(at_x[dx], at_y[dy]), device_id_type=MESH)
+    reaches = {1: has_right, -1: has_left}
+    hears = {1: has_left, -1: has_right}
+
+    def by_side(act, conditions):
+        act(0)
+        for side in (1, -1):
+            pl.when(conditions[side])(functools.partial(act, side))
+
+    def greet(side):
+        for dx, dy in DIRS:
+            if dx == side:
+                pl.semaphore_signal(
+                    barrier, inc=1, device_id=(at_x[dx], at_y[dy]), device_id_type=MESH
+                )
+
+    by_side(greet, reaches)
+
+    def start_all(copies):
+        def start(side):
+            for copy, (dx, dy) in zip(copies, DIRS):
+                if dx == side:
+                    copy.start()
+
+        by_side(start, reaches)
+
+    def wait_all(copies):
+        def sent(side):
+            for copy, (dx, dy) in zip(copies, DIRS):
+                if dx == side:
+                    copy.wait_send()
+
+        def received(side):
+            for copy, (dx, dy) in zip(copies, DIRS):
+                if dx == side:
+                    copy.wait_recv()
+
+        by_side(received, hears)
+        by_side(sent, reaches)
+
+    def start_to(side, copy):
+        if side == 0:
+            copy.start()
+        else:
+            pl.when(reaches[side])(copy.start)
+
+    def wait_to(side, copy):
+        if side == 0:
+            copy.wait()
+        else:
+            pl.when(hears[side])(copy.wait_recv)
+            pl.when(reaches[side])(copy.wait_send)
     for digits in stages:
         for k in range(1, members(digits)):
             pl.semaphore_signal(barrier, inc=1, device_id=partner(digits, k), device_id_type=MESH)
@@ -253,7 +302,8 @@
         for ey in range(EY):
             basis[ex, ey] = basis[ex, ey] * (scale_x[ex] * scale_y[ey])
 
-    pl.semaphore_wait(barrier, 8 + sum(members(d) - 1 for d in stages))
+    sides = 1 - (px + 1) // nx + (px + nx - 1) // nx
+    pl.semaphore_wait(barrier, 2 + 3 * sides + sum(members(d) - 1 for d in stages))
 
     field_copies = []
     for n, (dx, dy) in enumerate(DIRS):
@@ -268,7 +318,7 @@
                 f_send.at[n], f_recv.at[n], (at_x[dx], at_y[dy]),
             )
         )
-        field_copies[-1].start()
+    start_all(field_copies)
     up_copies = [
         remote(basis.at[EDGE[n], r], strip_y.at[n, r], y_send.at[t], y_recv.at[t], (px, lower))
         for t, (n, r) in enumerate(UP)
@@ -288,7 +338,7 @@
 
     feed(0)
     x_copy = remote(basis.at[pl.ds(0, 3)], strip_x, x_send, x_recv, (left, py))
-    x_copy.start()
+    start_to(-1, x_copy)
 
     empty = jnp.zeros((VEC, CZ), F32)
     for j in range(7):
@@ -302,8 +352,7 @@
 
     lax.fori_loop(1, 11, zero_rows, 0)
 
-    for copy in field_copies:
-        copy.wait()
+    wait_all(field_copies)
 
     @pl.when(px == 0)
     def _():
@@ -374,16 +423,15 @@
             return carry
 
         lax.fori_loop(0, EX, spread, 0, unroll=True)
-        for copy in halos[step]:
-            copy.start()
+        start_all(halos[step])
 
     exists = {(1, 0): has_left, (-1, 0): has_right, (0, 1): has_down, (0, -1): has_up}
 
     def gather_back(step):
         whole[...] = jnp.zeros((12, 7, 1, CZ), F32)
         whole[1:11, 1:6] = spread_out[step]
+        wait_all(halos[step])
         for n, (dx, dy) in enumerate(DIRS):
-            halos[step][n].wait()
             lx, tx = HALO_X[dx][1:]
             ly, ty = HALO_Y[dy][1:]
             there = exists[dx, 0] if dy == 0 else exists[0, dy] if dx == 0 else exists[dx, 0] & exists[0, dy]
@@ -442,6 +490,21 @@
     for j in range(1, 6):
         image[11, j] = -(field[11, j, 0:1, :] * weighted[10, j])
     feed(1)
+    two, rest = pl.ds(0, 2), pl.ds(4, 2)
+    tall = pl.ds(4, 3)
+    corner_copies = [
+        (side, remote(src, dst, c_send.at[n], c_recv.at[n], (to, py)))
+        for n, (side, src, dst, to) in enumerate(
+            (
+                (1, image.at[pl.ds(9, 2), tall], corner_r.at[two], right),
+                (1, image.at[11, rest], corner_r.at[2, two], right),
+                (-1, image.at[pl.ds(1, 2), tall], corner_l.at[pl.ds(1, 2)], left),
+                (-1, image.at[0, rest], corner_l.at[0, two], left),
+            )
+        )
+    ]
+    for side, copy in corner_copies:
+        start_to(side, copy)
 
     columns.append(gather_back(0))
     send_spread(1, columns[1])
@@ -456,16 +519,16 @@
     rows[4] = fold(lax.fori_loop(0, 5, own_block, jnp.zeros((2 * VEC, 2 * VEC), F32)))
     feed(2)
 
-    def send_block(n, block, to):
+    def send_block(n, block, to, side=0):
         block_out[n] = squeeze_block(block)
         copy = remote(block_out.at[n], block_in.at[n], b_send.at[n], b_recv.at[n], to)
-        copy.start()
-        return copy
+        start_to(side, copy)
+        return side, copy
 
     columns.append(gather_back(1))
     send_spread(2, columns[2])
 
-    x_copy.wait()
+    wait_to(-1, x_copy)
     block_x = fold(
         dot_cells(
             [image[9 + k, 1 + j] for k in range(3) for j in range(EY)],
@@ -473,23 +536,9 @@
         )
     )
     rows[7] = jnp.where(has_right, block_x, 0.0)
-    block_copies = [send_block(0, block_x.T, (right, py))]
+    block_copies = [send_block(0, block_x.T, (right, py), 1)]
     feed(3)
 
-    corner_copies = {}
-
-    def hand_on(n):
-        for t in range(len(UP)):
-            if UP[t][0] == n:
-                up_copies[t].wait()
-        part = pl.ds(0, 2 if n in (2, 3) else 3)
-        inbox, to = (corner_r.at[n], left) if n < 3 else (corner_l.at[n - 3], right)
-        copy = remote(strip_y.at[n, part], inbox.at[part], c_send.at[n], c_recv.at[n], (to, py))
-        copy.start()
-        corner_copies[n] = copy
-
-    hand_on(0)
-    hand_on(5)
     columns.append(gather_back(2))
 
     blank = jnp.zeros((1, CZ - VEC), F32)
@@ -531,8 +580,6 @@
 
     tell(0)
     feed(4)
-    hand_on(1)
-    hand_on(4)
     value = hear(0)
     tell(1)
     for copy in down_copies:
@@ -541,32 +588,30 @@
         dot_cells([strip_m[t] for t in range(len(DOWN))], [basis[c, r] for c, r in DOWN])
     )
     block_copies.append(send_block(1, part_m, (px, lower)))
-    hand_on(2)
-    hand_on(3)
+    for copy in up_copies:
+        copy.wait()
     part_e = fold(
         dot_cells(
             [image[EDGE[n] + 1, 4 + r] for n, r in UP], [strip_y[n, r] for n, r in UP]
         )
     )
     block_copies.append(send_block(2, part_e.T, (px, upper)))
-    for n in range(3):
-        corner_copies[n].wait()
+    for side, copy in corner_copies:
+        wait_to(side, copy)
+    block_l = fold(
+        dot_cells(
+            [corner_r[n, r] for n, r in UP if n < 3], [strip_y[n, r] for n, r in UP if n < 3]
+        )
+    )
+    block_copies.append(send_block(3, block_l.T, (px, upper)))
+    block_copies.append(send_block(5, block_l, (left, py), -1))
     block_r = fold(
         dot_cells(
-            [image[9 + n, 4 + r] for n, r in UP if n < 3],
-            [corner_r[n, r] for n, r in UP if n < 3],
-        )
-    )
-    block_copies.append(send_block(3, block_r.T, (right, upper)))
-    for n in range(3, 6):
-        corner_copies[n].wait()
-    block_l = fold(
-        dot_cells(
-            [image[n - 3, 4 + r] for n, r in UP if n > 2],
-            [corner_l[n - 3, r] for n, r in UP if n > 2],
-        )
-    )
-    block_copies.append(send_block(4, block_l.T, (left, upper)))
+            [corner_l[n - 3, r] for n, r in UP if n > 2], [strip_y[n, r] for n, r in UP if n > 2]
+        )
+    )
+    block_copies.append(send_block(4, block_r.T, (px, upper)))
+    block_copies.append(send_block(6, block_r, (right, py), 1))
     value = hear(1)
     tell(2)
     value = hear(2)
@@ -574,14 +619,14 @@
     found = SHRINK * (steps[0] * vectors[0] + steps[1] * vectors[1] + steps[2] * vectors[2])
     answer[0] = found[:, 0:VEC]
 
-    rows[8] = jnp.where(has_right & has_up, block_r, 0.0)
-    rows[2] = jnp.where(has_left & has_up, block_l, 0.0)
-    for copy in block_copies:
-        copy.wait()
+    for side, copy in block_copies:
+        wait_to(side, copy)
     rows[1] = jnp.where(has_left, spread_block(block_in[0]), 0.0)
     rows[5] = jnp.where(has_up, part_e + spread_block(block_in[1]), 0.0)
     rows[3] = jnp.where(has_down, part_m.T + spread_block(block_in[2]), 0.0)
     rows[0] = jnp.where(has_left & has_down, spread_block(block_in[3]), 0.0)
+    rows[8] = jnp.where(has_right & has_up, spread_block(block_in[5]), 0.0)
+    rows[2] = jnp.where(has_left & has_up, spread_block(block_in[6]), 0.0)
     rows[6] = jnp.where(has_right & has_down, spread_block(block_in[4]), 0.0)
 
 
@@ -613,15 +658,15 @@
             pltpu.VMEM((len(DOWN), VEC, CZ), F32),
             pltpu.VMEM((3, 3, VEC, CZ), F32),
             pltpu.VMEM((3, 3, VEC, CZ), F32),
-            pltpu.VMEM((5, 8, CZ), F32),
-            pltpu.VMEM((5, 8, CZ), F32),
+            pltpu.VMEM((7, 8, CZ), F32),
+            pltpu.VMEM((7, 8, CZ), F32),
             pltpu.VMEM((ITERS, EX, EY, 1, CZ), F32),
             pltpu.VMEM((ITERS, 8, EX, EY, 1, CZ), F32),
             pltpu.VMEM((12, 7, 1, CZ), F32),
             pltpu.VMEM((12, 7, 1, CZ), F32),
             pltpu.VMEM((len(stages), 2, CZ), F32),
             dma((3,)), dma((8,)), dma((8,)), dma((16,)), dma((16,)), dma, dma,
-            dma((14,)), dma((14,)), dma((6,)), dma((6,)), dma((5,)), dma((5,)),
+            dma((14,)), dma((14,)), dma((4,)), dma((4,)), dma((7,)), dma((7,)),
             dma((ITERS, 8)), dma((ITERS, 8)), dma((len(stages),)), dma((len(stages),)),
             *[pltpu.VMEM((members(digits) - 1, 2, CZ), F32) for digits in stages],
         ],

time: 76.2 us -> 73.6 us (0.966)
  Pallas kernels: 70.9 us -> 68.2 us
    pallas_call x1, Pallas kernels: 70.9 us -> 68.2 us  [body(): pl.pallas_call(functools.partial(kernel, nx, ny), out_shape=(jax.ShapeDty...]
where the time goes in v4:
time: 73.6 us; the launch traced here: 73.2 us
  Pallas kernels  68.2 us (93%)
  local copies, waits for them, and re-layouts  4.38 us (6%)
    pallas_call x1, Pallas kernels, body(): pl.pallas_call(functools.partial(kernel, nx, ny), out_shape=(jax.ShapeDty...  68.2 us
    unnamed x10, local copies, waits for them, and re-layouts  4.38 us

profile of v4, /device:TPU:1, one launch (start us, length us, event | category | flops | bytes accessed | tf_op | source)
XLA Modules:
  0.0 73.2 jit_solution(7181088780235057048)
XLA Ops:
  0.6 0.0 copy-start.3
  0.6 0.6 copy-done.3
  1.3 0.0 copy-start
  1.3 1.1 %copy-done = f32[32,10,5,128]{3,0,2,1:T(8,128)S(1)} copy-done((f32[32,10,5,128]{3,0,2,1:T(8,128)S(1)}, f32[32,10,5,128]{3,0,2,1:T(8,128)}, u32[]{:S(2)}) %copy-start) | copy-done | bytes 819224
  2.4 0.0 copy-start.1
  2.4 0.7 copy-done.1
  3.1 0.0 copy-start.2
  3.1 0.7 copy-done.2
  3.8 68.2 %coarse.1 = (f32[9,32,32]{2,1,0:T(8,128)S(1)}, f32[1,1,32]{2,1,0:T(1,128)S(1)}) custom-call(f32[10,5,32,128]{3,2,1,0:T(8,128)S(1)} %bitcast.4, s32[3,8,128]{2,1,0:T(8,128)S(1)} %bitcast.6, f32[85]{0:T(128)S(1)} %copy-done.3, f32[3,8,128]{2,1,0:T(8,128)S(1)} %bitcast.7), custom_call_target="tpu_custom_call" | custom-call | tf_op jit(solution)/shard_map/coarse/pallas_call | solution.py:640
  72.0 0.7 copy.8
  72.7 0.5 copy.9
Async XLA Ops:
  0.6 0.7 copy-start.3
  1.3 1.1 %copy-start = (f32[32,10,5,128]{3,0,2,1:T(8,128)S(1)}, f32[32,10,5,128]{3,0,2,1:T(8,128)}, u32[]{:S(2)}) copy-start(f32[32,10,5,128]{3,0,2,1:T(8,128)} %param.4) | copy-start | bytes 2457604
  2.4 0.7 copy-start.1
  3.1 0.7 copy-start.2

commit v5 on v4

--- a/solution.py
+++ b/solution.py
@@ -503,8 +503,6 @@
             )
         )
     ]
-    for side, copy in corner_copies:
-        start_to(side, copy)
 
     columns.append(gather_back(0))
     send_spread(1, columns[1])
@@ -538,6 +536,8 @@
     rows[7] = jnp.where(has_right, block_x, 0.0)
     block_copies = [send_block(0, block_x.T, (right, py), 1)]
     feed(3)
+    for side, copy in corner_copies:
+        start_to(side, copy)
 
     columns.append(gather_back(2))
 

time: 73.6 us -> 72.9 us (level)
  no operation moved by 1% of the time
where the time goes in v5:
time: 72.9 us; the launch traced here: 72.6 us
  Pallas kernels  67.6 us (93%)
  local copies, waits for them, and re-layouts  4.38 us (6%)
    pallas_call x1, Pallas kernels, body(): pl.pallas_call(functools.partial(kernel, nx, ny), out_shape=(jax.ShapeDty...  67.6 us
    unnamed x10, local copies, waits for them, and re-layouts  4.38 us

profile of v5, /device:TPU:1, one launch (start us, length us, event | category | flops | bytes accessed | tf_op | source)
XLA Modules:
  0.0 72.6 jit_solution(12157629066722374235)
XLA Ops:
  0.6 0.0 copy-start.3
  0.6 0.6 copy-done.3
  1.3 0.0 copy-start
  1.3 1.1 %copy-done = f32[32,10,5,128]{3,0,2,1:T(8,128)S(1)} copy-done((f32[32,10,5,128]{3,0,2,1:T(8,128)S(1)}, f32[32,10,5,128]{3,0,2,1:T(8,128)}, u32[]{:S(2)}) %copy-start) | copy-done | bytes 819224
  2.4 0.0 copy-start.1
  2.4 0.7 copy-done.1
  3.1 0.0 copy-start.2
  3.1 0.7 copy-done.2
  3.8 67.6 %coarse.1 = (f32[9,32,32]{2,1,0:T(8,128)S(1)}, f32[1,1,32]{2,1,0:T(1,128)S(1)}) custom-call(f32[10,5,32,128]{3,2,1,0:T(8,128)S(1)} %bitcast.4, s32[3,8,128]{2,1,0:T(8,128)S(1)} %bitcast.6, f32[85]{0:T(128)S(1)} %copy-done.3, f32[3,8,128]{2,1,0:T(8,128)S(1)} %bitcast.7), custom_call_target="tpu_custom_call" | custom-call | tf_op jit(solution)/shard_map/coarse/pallas_call | solution.py:640
  71.4 0.7 copy.8
  72.1 0.5 copy.9
Async XLA Ops:
  0.6 0.7 copy-start.3
  1.3 1.1 %copy-start = (f32[32,10,5,128]{3,0,2,1:T(8,128)S(1)}, f32[32,10,5,128]{3,0,2,1:T(8,128)}, u32[]{:S(2)}) copy-start(f32[32,10,5,128]{3,0,2,1:T(8,128)} %param.4) | copy-start | bytes 2457604
  2.4 0.7 copy-start.1
  3.1 0.7 copy-start.2
